TPU v7x, 128 devices: a whole 4x4x4 slice. The times are simulated.
128 devices in a mesh: ang: 32 (over y, x, z_lo), ax: 4 (over z_hi, core).
Axes of the slice: x: 4, y: 4, z: 4 (z_hi: 2, z_lo: 2; z = z_hi * 2 + z_lo), core: 2. Of those that a mesh axis runs over, the one named last changes fastest.
Arguments:
- conserved: float32 [5, 96, 1024, 256], P(None, 'ax', 'ang'), may hold values from -0.3 to 3.5, as said below
- deriv_matrix: float32 [512, 512], replicated, may hold values from -1 to 1
- filter_matrix: float32 [512, 512], replicated, may hold values from 0 to 1
Outputs:
- advanced: float32 [5, 96, 1024, 256], P(None, 'ax', 'ang')
Inputs may be any that keep to these rules, and one draw needn't show every extreme that they name: `conserved`: component 0 (density) lies in 0.8 to 1.2, components 1 to 3 (momenta) in -0.3 to 0.3, and the energy exceeds the kinetic energy by 1.75 to 3.25.
All inputs are finite; a program needn't handle non-finite values.
Results may differ from a plain program's by a relative error of at most 0.0003.
Values sent between devices are 32-bit elements; how exact they have to be, the bound alone decides.
A program may use at most 128 MiB of HBM per device.

v0:
```python
import math

import jax
import jax.numpy as jnp
from jax import lax
from jax.experimental import pallas as pl
from jax.experimental.pallas import tpu as pltpu
from jax.sharding import PartitionSpec as P

MESH = pl.DeviceIdType.MESH
COURANT = 0.15
GROUP = 2
FIELDS = 5
BLOCK = 16
PAD = 8

ARRIVE, FIRST, SECOND = 0, 1, 2


def step_list(chunks):
    order = [chunks - 1] + list(range(chunks - 1))
    steps, here, first, second = [], set(), [], []

    def ready(chunk, done):
        return all(n in done for n in (chunk - 1, chunk, chunk + 1) if 0 <= n < chunks)

    for place, chunk in enumerate(order):
        steps.append((ARRIVE, chunk))
        here.add(chunk)
        for c in range(chunks):
            if c not in first and ready(c, here):
                steps.append((FIRST, c))
                first.append(c)
        for c in range(1, chunks - 1):
            if place < chunks - 1 and c not in second and ready(c, first):
                steps.append((SECOND, c))
                second.append(c)
    late = [c for c in range(1, chunks) if c not in second] + [0]
    return order, steps + [(SECOND, c) for c in late]


def chosen(step, values):
    total = jnp.int32(0)
    for i, value in enumerate(values):
        if value:
            total = total + jnp.where(step == i, jnp.int32(value), jnp.int32(0))
    return total


def split(value):
    high = value.astype(jnp.bfloat16)
    low = (value - high.astype(jnp.float32)).astype(jnp.bfloat16)
    return high, low


def dot(a, b):
    return jnp.dot(a, b, preferred_element_type=jnp.float32)


def jet_kernel(
    n_ang, n_ax, x_ref, deriv_ref, filt_ref, out_ref,
    state, operand_hi, operand_lo, angular, axial, edge_out, edge_in,
    mats, table, gain_hi, gain_lo,
    in_s, in_r, edge_s, edge_r, ax_s, ax_r, out_s, out_r, mat_s,
):
    planes, lines, radii = x_ref.shape[1:]
    own = planes // 2
    chunks = own // GROUP
    half = n_ang // 2
    n_hi = n_ax // 2
    order, steps = step_list(chunks)

    ang = lax.axis_index("ang")
    ax = lax.axis_index("ax")
    core = lax.rem(ax, 2)
    z_hi = lax.div(ax, 2)
    side = lax.div(ang, half)
    place = lax.rem(ang, half)
    keep = lax.rem(side + z_hi, 2)
    is_keeper = core == keep
    is_giver = core != keep
    across = lax.rem(ang + half, n_ang)
    sibling = (ang, 2 * z_hi + 1 - core)
    left = (side * half + lax.rem(place + half - 1, half), ax)
    right = (side * half + lax.rem(place + 1, half), ax)

    low_sib = core == 1
    low_far = (core == 0) & (keep == 1)
    low_z = (core == 0) & (keep == 0) & (z_hi > 0)
    has_low = low_sib | low_far | low_z
    low_dev = (
        jnp.where(low_far, across, ang),
        jnp.where(low_sib, ax - 1, jnp.where(low_far, 2 * z_hi + 1, 2 * z_hi - 1)),
    )
    up_sib = core == 0
    up_far = (core == 1) & (keep == 0)
    up_z = (core == 1) & (keep == 1) & (z_hi < n_hi - 1)
    has_up = up_sib | up_far | up_z
    up_dev = (
        jnp.where(up_far, across, ang),
        jnp.where(up_sib, ax + 1, jnp.where(up_far, 2 * z_hi, 2 * z_hi + 2)),
    )

    def load_mats():
        return [
            pltpu.make_async_copy(filt_ref, mats.at[0], mat_s.at[0]),
            pltpu.make_async_copy(deriv_ref, mats.at[1], mat_s.at[1]),
        ]

    def group(start):
        return pl.ds(start, GROUP)

    def give(target, chunk):
        return pltpu.make_async_remote_copy(
            src_ref=x_ref.at[:, group(own * target + GROUP * chunk)],
            dst_ref=state.at[0, side, :, group(GROUP * chunk)],
            send_sem=in_s.at[target, chunk],
            recv_sem=in_r.at[1, chunk],
            device_id=(across, 2 * z_hi + target),
            device_id_type=MESH,
        )

    def share(chunk):
        return pltpu.make_async_remote_copy(
            src_ref=x_ref.at[:, group(own * (1 - core) + GROUP * chunk)],
            dst_ref=state.at[0, side, :, group(GROUP * chunk)],
            send_sem=in_s.at[0, chunk],
            recv_sem=in_r.at[0, chunk],
            device_id=sibling,
            device_id_type=MESH,
        )

    def hold(chunk):
        return pltpu.make_async_copy(
            x_ref.at[:, group(own * core + GROUP * chunk)],
            state.at[0, side, :, group(GROUP * chunk)],
            in_r.at[0, chunk],
        )

    def wait_for(ref, sem):
        pltpu.make_async_copy(ref, ref, sem).wait()

    def edge_copy(which, slot):
        return pltpu.make_async_remote_copy(
            src_ref=edge_out.at[slot, which],
            dst_ref=edge_in.at[slot, 1 - which],
            send_sem=edge_s.at[slot, which],
            recv_sem=edge_r.at[slot, 1 - which],
            device_id=left if which == 0 else right,
            device_id_type=MESH,
        )

    def axial_copy(which, stage):
        if which == 0:
            source, target, device = 2, own + 2, low_dev
        else:
            source, target, device = own, 0, up_dev
        return pltpu.make_async_remote_copy(
            src_ref=axial.at[stage, :, :, pl.ds(source, 2)],
            dst_ref=axial.at[stage, :, :, pl.ds(target, 2)],
            send_sem=ax_s.at[stage, which],
            recv_sem=ax_r.at[stage, 1 - which],
            device_id=device,
            device_id_type=MESH,
        )

    def out_planes(chunk):
        return out_ref.at[:, group(own * core + GROUP * chunk)]

    def out_far(chunk):
        return pltpu.make_async_remote_copy(
            src_ref=state.at[2, 1 - side, :, group(GROUP * chunk)],
            dst_ref=out_planes(chunk),
            send_sem=out_s.at[0, chunk],
            recv_sem=out_r.at[core, chunk],
            device_id=(across, 2 * z_hi + keep),
            device_id_type=MESH,
        )

    def out_near(chunk):
        return pltpu.make_async_remote_copy(
            src_ref=state.at[2, side, :, group(GROUP * chunk)],
            dst_ref=out_planes(chunk),
            send_sem=out_s.at[1, chunk],
            recv_sem=out_r.at[core, chunk],
            device_id=sibling,
            device_id_type=MESH,
        )

    def out_here(chunk):
        return pltpu.make_async_copy(
            state.at[2, side, :, group(GROUP * chunk)], out_planes(chunk), out_r.at[core, chunk]
        )

    barrier = pltpu.get_barrier_semaphore()
    for device in (sibling, (across, 2 * z_hi), (across, 2 * z_hi + 1), left, right):
        pl.semaphore_signal(barrier, inc=1, device_id=device, device_id_type=MESH)

    @pl.when(low_z)
    def _():
        pl.semaphore_signal(barrier, inc=1, device_id=low_dev, device_id_type=MESH)

    @pl.when(up_z)
    def _():
        pl.semaphore_signal(barrier, inc=1, device_id=up_dev, device_id_type=MESH)

    pl.semaphore_wait(barrier, jnp.where(low_z | up_z, jnp.int32(6), jnp.int32(5)))

    @pl.when(is_giver)
    def _():
        for chunk in order:
            for target in range(2):
                give(target, chunk).start()

    @pl.when(is_keeper)
    def _():
        for chunk in order:
            hold(chunk).start()
            share(chunk).start()

    for copy in load_mats():
        copy.start()

    ends = jnp.zeros((2, 2, FIELDS, 2, lines, radii), jnp.float32)

    @pl.when(jnp.logical_not(has_low))
    def _():
        axial[:, :, :, 0:2] = ends

    @pl.when(jnp.logical_not(has_up))
    def _():
        axial[:, :, :, own + 2 : own + 4] = ends

    for seg in range(2):
        line = lax.broadcasted_iota(jnp.int32, (lines, 128), 0)
        index = seg * (half * lines) + place * lines + line
        angle = index.astype(jnp.float32) * (2.0 * math.pi / (n_ang * lines))
        table[seg, 0] = jnp.cos(angle)
        table[seg, 1] = jnp.sin(angle)

    row = lax.broadcasted_iota(jnp.int32, (radii, radii), 0)
    column = lax.broadcasted_iota(jnp.int32, (radii, radii), 1)
    flip = jnp.where(row + column == radii - 1, 1.0, 0.0).astype(jnp.bfloat16)

    def arranged(part):
        low_rows = dot(flip, part[:radii]).astype(jnp.bfloat16)
        rows = jnp.concatenate([part[radii:], low_rows], axis=0)
        low_columns = dot(rows[:, :radii], flip).astype(jnp.bfloat16)
        return jnp.concatenate([rows[:, radii:], low_columns], axis=1)

    for copy in load_mats():
        copy.wait()
    filt_parts = [arranged(part) for part in split(mats[0].T)]
    deriv_parts = [arranged(part) for part in split(mats[1].T)]
    gain_hi[: 2 * radii] = filt_parts[0]
    gain_lo[: 2 * radii] = filt_parts[1]
    signed = [jnp.concatenate([part[:radii], -part[radii:]], axis=0) for part in filt_parts]
    both = (
        dot(deriv_parts[0], signed[0]) + dot(deriv_parts[1], signed[0]) + dot(deriv_parts[0], signed[1])
    )
    both_hi, both_lo = split(both)
    gain_hi[2 * radii :] = both_hi
    gain_lo[2 * radii :] = both_lo

    radius = (
        lax.broadcasted_iota(jnp.int32, (BLOCK, radii), 1).astype(jnp.float32) + 0.5
    ) / radii
    twist = n_ang * lines / (2.0 * math.pi * radii)
    wide = radii // 128

    def fluxes(stage, chunk):
        factor = (1.0 - 0.5 * stage.astype(jnp.float32)) * COURANT
        scaled_radius = radius * (-factor)

        def one(item, carry):
            seg = lax.div(item, GROUP)
            sub = lax.rem(item, GROUP)
            plane = GROUP * chunk + sub
            for r0 in range(0, lines, BLOCK):
                rows = pl.ds(r0, BLOCK)
                density, x_mom, y_mom, z_mom, energy = [
                    state[stage, seg, k, plane, rows, :] for k in range(FIELDS)
                ]
                cosine = jnp.concatenate([table[seg, 0, rows, :]] * wide, axis=1)
                sine = jnp.concatenate([table[seg, 1, rows, :]] * wide, axis=1)
                inverse = 1.0 / density
                x_speed = x_mom * inverse
                y_speed = y_mom * inverse
                z_speed = z_mom * inverse
                pressure = 0.4 * (
                    energy - 0.5 * (x_mom * x_speed + y_mom * y_speed + z_mom * z_speed)
                )
                radial_speed = x_speed * cosine + y_speed * sine
                swirl_speed = y_speed * cosine - x_speed * sine
                enthalpy = energy + pressure
                pressure_cos = pressure * cosine
                pressure_sin = pressure * sine
                radial = (
                    density * radial_speed,
                    x_mom * radial_speed + pressure_cos,
                    y_mom * radial_speed + pressure_sin,
                    z_mom * radial_speed,
                    enthalpy * radial_speed,
                )
                around = (
                    density * swirl_speed,
                    x_mom * swirl_speed - pressure_sin,
                    y_mom * swirl_speed + pressure_cos,
                    z_mom * swirl_speed,
                    enthalpy * swirl_speed,
                )
                along = (
                    z_mom,
                    x_mom * z_speed,
                    y_mom * z_speed,
                    z_mom * z_speed + pressure,
                    enthalpy * z_speed,
                )
                columns = pl.ds(pl.multiple_of((2 + seg) * radii, 128), radii)
                for k in range(FIELDS):
                    high, low = split(radial[k] * scaled_radius)
                    operand_hi[chunk, k, sub, rows, columns] = high
                    operand_lo[chunk, k, sub, rows, columns] = low
                    angular[chunk, seg, k, sub, pl.ds(PAD + r0, BLOCK), :] = around[k]
                    axial[stage, seg, k, 2 + plane, rows, :] = along[k]
            slot = stage * chunks + chunk
            for k in range(FIELDS):
                edge_out[slot, 0, seg, k, sub] = angular[chunk, seg, k, sub, pl.ds(PAD, 2), :]
                edge_out[slot, 1, seg, k, sub] = angular[
                    chunk, seg, k, sub, pl.ds(PAD + lines - 2, 2), :
                ]
            return carry

        lax.fori_loop(0, 2 * GROUP, one, 0)
        slot = stage * chunks + chunk
        edge_copy(0, slot).start()
        edge_copy(1, slot).start()

        @pl.when((chunk == 0) & has_low)
        def _():
            axial_copy(0, stage).start()

        @pl.when((chunk == chunks - 1) & has_up)
        def _():
            axial_copy(1, stage).start()

    def advance(stage, chunk):
        slot = stage * chunks + chunk
        wait_for(edge_in.at[slot, 0], edge_r.at[slot, 0])
        wait_for(edge_in.at[slot, 1], edge_r.at[slot, 1])

        @pl.when((chunk == 0) & has_low)
        def _():
            wait_for(axial.at[stage, :, :, pl.ds(0, 2)], ax_r.at[stage, 0])

        @pl.when((chunk == chunks - 1) & has_up)
        def _():
            wait_for(axial.at[stage, :, :, pl.ds(own + 2, 2)], ax_r.at[stage, 1])

        factor = (1.0 - 0.5 * stage.astype(jnp.float32)) * COURANT
        turn_near = factor * (twist * 8.0 / 12.0)
        turn_far = factor * (twist / 12.0)
        scaled_near = radius * (factor * (8.0 / 12.0))
        scaled_far = radius * (factor * (1.0 / 12.0))
        swap_low = jnp.where(place == 0, jnp.int32(1), jnp.int32(0))
        swap_up = jnp.where(place == half - 1, jnp.int32(1), jnp.int32(0))

        def one(item, carry):
            seg = lax.div(item, GROUP)
            sub = lax.rem(item, GROUP)
            plane = GROUP * chunk + sub
            seg_low = lax.rem(seg + swap_low, 2)
            seg_up = lax.rem(seg + swap_up, 2)
            for k in range(FIELDS):
                angular[chunk, seg, k, sub, pl.ds(PAD - 2, 2), :] = edge_in[slot, 0, seg_low, k, sub]
                angular[chunk, seg, k, sub, pl.ds(PAD + lines, 2), :] = edge_in[slot, 1, seg_up, k, sub]
            columns = pl.ds(pl.multiple_of(seg * radii, 128), radii)
            for r0 in range(0, lines, BLOCK):
                rows = pl.ds(r0, BLOCK)
                for k in range(FIELDS):
                    def beside(offset):
                        return angular[chunk, seg, k, sub, pl.ds(PAD + r0 + offset, BLOCK), :]

                    def above(offset):
                        return axial[stage, seg, k, 2 + plane + offset, rows, :]

                    base = 0.5 * state[0, seg, k, plane, rows, :] + 0.5 * state[stage, seg, k, plane, rows, :]
                    local = (
                        base
                        - (turn_near * (beside(1) - beside(-1)) - turn_far * (beside(2) - beside(-2)))
                        - (scaled_near * (above(1) - above(-1)) - scaled_far * (above(2) - above(-2)))
                    )
                    high, low = split(local)
                    operand_hi[chunk, k, sub, rows, columns] = high
                    operand_lo[chunk, k, sub, rows, columns] = low
            return carry

        lax.fori_loop(0, 2 * GROUP, one, 0)
        flat = (FIELDS * GROUP * lines, 4 * radii)
        high = operand_hi[chunk].reshape(flat)
        low = operand_lo[chunk].reshape(flat)
        result = dot(high, gain_hi[...]) + dot(low, gain_hi[...]) + dot(high, gain_lo[...])
        result = result.reshape(FIELDS, GROUP, lines, 2 * radii)
        for seg in range(2):
            state[stage + 1, seg, :, group(GROUP * chunk)] = result[..., seg * radii : (seg + 1) * radii]

    kinds = [kind for kind, _ in steps]
    which = [chunk for _, chunk in steps]

    def one_step(step, carry):
        kind = chosen(step, kinds)
        chunk = chosen(step, which)

        @pl.when(kind == ARRIVE)
        def _():
            here = state.at[0, 0, :, group(GROUP * chunk)]
            wait_for(here, in_r.at[0, chunk])
            wait_for(here, in_r.at[1, chunk])

        @pl.when(kind != ARRIVE)
        def _():
            advance(kind - FIRST, chunk)

        @pl.when(kind != SECOND)
        def _():
            fluxes(kind, chunk)

        @pl.when(kind == SECOND)
        def _():
            out_far(chunk).start()

            @pl.when(is_keeper)
            def _():
                out_here(chunk).start()

            @pl.when(is_giver)
            def _():
                out_near(chunk).start()

        return carry

    lax.fori_loop(0, len(steps), one_step, 0)

    def finish(chunk, carry):
        sample = state.at[0, 0, :, group(GROUP * chunk)]
        wait_for(sample, in_s.at[0, chunk])
        wait_for(sample, out_s.at[0, chunk])

        @pl.when(is_giver)
        def _():
            wait_for(sample, in_s.at[1, chunk])
            wait_for(sample, out_s.at[1, chunk])

        for stage in range(2):
            slot = stage * chunks + chunk
            wait_for(edge_out.at[slot, 0], edge_s.at[slot, 0])
            wait_for(edge_out.at[slot, 1], edge_s.at[slot, 1])
        for source in range(2):
            wait_for(sample, out_r.at[source, chunk])
        return carry

    lax.fori_loop(0, chunks, finish, 0)
    for stage in range(2):
        @pl.when(has_low)
        def _():
            wait_for(axial.at[stage, :, :, pl.ds(2, 2)], ax_s.at[stage, 0])

        @pl.when(has_up)
        def _():
            wait_for(axial.at[stage, :, :, pl.ds(own, 2)], ax_s.at[stage, 1])


def per_device(conserved, deriv_matrix, filter_matrix):
    n_ang = lax.axis_size("ang")
    n_ax = lax.axis_size("ax")
    _, planes, lines, radii = conserved.shape
    own = planes // 2
    chunks = own // GROUP
    f32, bf16 = jnp.float32, jnp.bfloat16
    anywhere = pl.BlockSpec(memory_space=pl.ANY)

    def kernel(*refs):
        jet_kernel(n_ang, n_ax, *refs)

    dma = pltpu.SemaphoreType.DMA
    return pl.pallas_call(
        kernel,
        out_shape=jax.ShapeDtypeStruct(conserved.shape, f32),
        in_specs=[anywhere] * 3,
        out_specs=anywhere,
        scratch_shapes=[
            pltpu.VMEM((3, 2, FIELDS, own, lines, radii), f32),
            pltpu.VMEM((chunks, FIELDS, GROUP, lines, 4 * radii), bf16),
            pltpu.VMEM((chunks, FIELDS, GROUP, lines, 4 * radii), bf16),
            pltpu.VMEM((chunks, 2, FIELDS, GROUP, lines + 2 * PAD, radii), f32),
            pltpu.VMEM((2, 2, FIELDS, own + 4, lines, radii), f32),
            pltpu.VMEM((2 * chunks, 2, 2, FIELDS, GROUP, 2, radii), f32),
            pltpu.VMEM((2 * chunks, 2, 2, FIELDS, GROUP, 2, radii), f32),
            pltpu.VMEM((2, 2 * radii, 2 * radii), f32),
            pltpu.VMEM((2, 2, lines, 128), f32),
            pltpu.VMEM((4 * radii, 2 * radii), bf16),
            pltpu.VMEM((4 * radii, 2 * radii), bf16),
            dma((2, chunks)),
            dma((2, chunks)),
            dma((2 * chunks, 2)),
            dma((2 * chunks, 2)),
            dma((2, 2)),
            dma((2, 2)),
            dma((2, chunks)),
            dma((2, chunks)),
            dma((2,)),
        ],
        compiler_params=pltpu.CompilerParams(
            collective_id=0, has_side_effects=True, vmem_limit_bytes=58 * 1024 * 1024
        ),
    )(conserved, deriv_matrix, filter_matrix)


def solution(mesh):
    spec = P(None, "ax", "ang", None)
    return jax.shard_map(
        per_device,
        mesh=mesh,
        in_specs=(spec, P(), P()),
        out_specs=spec,
        check_vma=False,
    )
```

profile of v0, /device:TPU:1, one launch (start us, length us, event | category | flops | bytes accessed | tf_op | source)
XLA Modules:
  0.0 128.9 jit_solution(17768999103950765877)
XLA Ops:
  0.0 124.3 %shard_map.37 = f32[5,24,32,256]{3,2,1,0:T(8,128)} custom-call(f32[5,24,32,256]{3,2,1,0:T(8,128)} %refs_0_.1, f32[512,512]{1,0:T(8,128)} %refs_1_.1, f32[512,512]{1,0:T(8,128)} %refs_2_.1), custom_call_target="tpu_custom_call" | custom-call | tf_op jit(solution)/shard_map/pallas_call | solution.py:486
  124.3 4.6 %copy.5 = f32[5,24,32,256]{3,2,1,0:T(8,128)} copy(f32[5,24,32,256]{3,2,1,0:T(8,128)} %shard_map.37) | data formatting | bytes 7864320
where the time goes:
time: 129 us
  Pallas kernels  124 us (96%)
  local copies, waits for them, and re-layouts  4.58 us (4%)
    pallas_call x1, Pallas kernels, per_device(): pl.pallas_call(kernel, out_shape=jax.ShapeDtypeStruct(conserved.shape, f3...  124 us
    unnamed x1, local copies, waits for them, and re-layouts  4.58 us

commit v1 on v0

--- a/solution.py
+++ b/solution.py
@@ -13,8 +13,10 @@
 FIELDS = 5
 BLOCK = 16
 PAD = 8
+SHIFT = 2 * GROUP
 
 ARRIVE, FIRST, SECOND = 0, 1, 2
+FAR, NEAR = 100, 101
 
 
 def step_list(chunks):
@@ -27,6 +29,8 @@
     for place, chunk in enumerate(order):
         steps.append((ARRIVE, chunk))
         here.add(chunk)
+        if place == 1:
+            steps += [(ARRIVE, FAR), (ARRIVE, NEAR), (FIRST, NEAR)]
         for c in range(chunks):
             if c not in first and ready(c, here):
                 steps.append((FIRST, c))
@@ -61,7 +65,7 @@
     n_ang, n_ax, x_ref, deriv_ref, filt_ref, out_ref,
     state, operand_hi, operand_lo, angular, axial, edge_out, edge_in,
     mats, table, gain_hi, gain_lo,
-    in_s, in_r, edge_s, edge_r, ax_s, ax_r, out_s, out_r, mat_s,
+    in_s, in_r, more_s, more_r, edge_s, edge_r, ax_s, ax_r, out_s, out_r, mat_s,
 ):
     planes, lines, radii = x_ref.shape[1:]
     own = planes // 2
@@ -87,19 +91,16 @@
     low_sib = core == 1
     low_far = (core == 0) & (keep == 1)
     low_z = (core == 0) & (keep == 0) & (z_hi > 0)
-    has_low = low_sib | low_far | low_z
-    low_dev = (
-        jnp.where(low_far, across, ang),
-        jnp.where(low_sib, ax - 1, jnp.where(low_far, 2 * z_hi + 1, 2 * z_hi - 1)),
-    )
+    has_low = low_sib | low_z
+    low_dev = (ang, ax - 1)
     up_sib = core == 0
     up_far = (core == 1) & (keep == 0)
     up_z = (core == 1) & (keep == 1) & (z_hi < n_hi - 1)
-    has_up = up_sib | up_far | up_z
-    up_dev = (
-        jnp.where(up_far, across, ang),
-        jnp.where(up_sib, ax + 1, jnp.where(up_far, 2 * z_hi, 2 * z_hi + 2)),
-    )
+    has_up = up_sib | up_z
+    up_dev = (ang, ax + 1)
+    near = jnp.where(core == 0, jnp.int32(-1), jnp.int32(chunks))
+    far = jnp.where(core == 0, jnp.int32(-2), jnp.int32(chunks + 1))
+    more = 2 * GROUP
 
     def load_mats():
         return [
@@ -110,10 +111,13 @@
     def group(start):
         return pl.ds(start, GROUP)
 
+    def within(chunk):
+        return pl.ds(GROUP * chunk + SHIFT, GROUP)
+
     def give(target, chunk):
         return pltpu.make_async_remote_copy(
             src_ref=x_ref.at[:, group(own * target + GROUP * chunk)],
-            dst_ref=state.at[0, side, :, group(GROUP * chunk)],
+            dst_ref=state.at[0, side, :, within(chunk)],
             send_sem=in_s.at[target, chunk],
             recv_sem=in_r.at[1, chunk],
             device_id=(across, 2 * z_hi + target),
@@ -123,7 +127,7 @@
     def share(chunk):
         return pltpu.make_async_remote_copy(
             src_ref=x_ref.at[:, group(own * (1 - core) + GROUP * chunk)],
-            dst_ref=state.at[0, side, :, group(GROUP * chunk)],
+            dst_ref=state.at[0, side, :, within(chunk)],
             send_sem=in_s.at[0, chunk],
             recv_sem=in_r.at[0, chunk],
             device_id=sibling,
@@ -133,8 +137,28 @@
     def hold(chunk):
         return pltpu.make_async_copy(
             x_ref.at[:, group(own * core + GROUP * chunk)],
-            state.at[0, side, :, group(GROUP * chunk)],
+            state.at[0, side, :, within(chunk)],
             in_r.at[0, chunk],
+        )
+
+    first_more = jnp.where(core == 0, jnp.int32(planes - more), jnp.int32(0))
+    place_more = jnp.where(core == 0, jnp.int32(0), jnp.int32(SHIFT + own))
+
+    def more_here():
+        return pltpu.make_async_copy(
+            x_ref.at[:, pl.ds(first_more, more)],
+            state.at[0, side, :, pl.ds(place_more, more)],
+            more_r.at[0],
+        )
+
+    def more_across():
+        return pltpu.make_async_remote_copy(
+            src_ref=x_ref.at[:, pl.ds(first_more, more)],
+            dst_ref=state.at[0, side, :, pl.ds(place_more, more)],
+            send_sem=more_s.at[0],
+            recv_sem=more_r.at[1],
+            device_id=(across, ax),
+            device_id_type=MESH,
         )
 
     def wait_for(ref, sem):
@@ -152,9 +176,9 @@
 
     def axial_copy(which, stage):
         if which == 0:
-            source, target, device = 2, own + 2, low_dev
+            source, target, device = SHIFT, SHIFT + own, low_dev
         else:
-            source, target, device = own, 0, up_dev
+            source, target, device = SHIFT + own - 2, SHIFT - 2, up_dev
         return pltpu.make_async_remote_copy(
             src_ref=axial.at[stage, :, :, pl.ds(source, 2)],
             dst_ref=axial.at[stage, :, :, pl.ds(target, 2)],
@@ -169,7 +193,7 @@
 
     def out_far(chunk):
         return pltpu.make_async_remote_copy(
-            src_ref=state.at[2, 1 - side, :, group(GROUP * chunk)],
+            src_ref=state.at[0, 1 - side, :, within(chunk)],
             dst_ref=out_planes(chunk),
             send_sem=out_s.at[0, chunk],
             recv_sem=out_r.at[core, chunk],
@@ -179,7 +203,7 @@
 
     def out_near(chunk):
         return pltpu.make_async_remote_copy(
-            src_ref=state.at[2, side, :, group(GROUP * chunk)],
+            src_ref=state.at[0, side, :, within(chunk)],
             dst_ref=out_planes(chunk),
             send_sem=out_s.at[1, chunk],
             recv_sem=out_r.at[core, chunk],
@@ -189,7 +213,7 @@
 
     def out_here(chunk):
         return pltpu.make_async_copy(
-            state.at[2, side, :, group(GROUP * chunk)], out_planes(chunk), out_r.at[core, chunk]
+            state.at[0, side, :, within(chunk)], out_planes(chunk), out_r.at[core, chunk]
         )
 
     barrier = pltpu.get_barrier_semaphore()
@@ -208,28 +232,32 @@
 
     @pl.when(is_giver)
     def _():
-        for chunk in order:
+        for turn, chunk in enumerate(order):
             for target in range(2):
                 give(target, chunk).start()
+            if turn == 1:
+                more_here().start()
 
     @pl.when(is_keeper)
     def _():
-        for chunk in order:
+        for turn, chunk in enumerate(order):
             hold(chunk).start()
             share(chunk).start()
+            if turn == 1:
+                more_across().start()
 
     for copy in load_mats():
         copy.start()
 
     ends = jnp.zeros((2, 2, FIELDS, 2, lines, radii), jnp.float32)
 
-    @pl.when(jnp.logical_not(has_low))
-    def _():
-        axial[:, :, :, 0:2] = ends
-
-    @pl.when(jnp.logical_not(has_up))
-    def _():
-        axial[:, :, :, own + 2 : own + 4] = ends
+    @pl.when(jnp.logical_not(has_low | low_far))
+    def _():
+        axial[:, :, :, SHIFT - 2 : SHIFT] = ends
+
+    @pl.when(jnp.logical_not(has_up | up_far))
+    def _():
+        axial[:, :, :, SHIFT + own : SHIFT + own + 2] = ends
 
     for seg in range(2):
         line = lax.broadcasted_iota(jnp.int32, (lines, 128), 0)
@@ -268,14 +296,22 @@
     twist = n_ang * lines / (2.0 * math.pi * radii)
     wide = radii // 128
 
+    def held_at(chunk):
+        return jnp.clip(chunk, -1, chunks) + 1
+
+    def slot_of(stage, chunk):
+        return stage * (chunks + 2) + held_at(chunk)
+
     def fluxes(stage, chunk):
+        held = held_at(chunk)
+        slot = slot_of(stage, chunk)
         factor = (1.0 - 0.5 * stage.astype(jnp.float32)) * COURANT
         scaled_radius = radius * (-factor)
 
         def one(item, carry):
             seg = lax.div(item, GROUP)
             sub = lax.rem(item, GROUP)
-            plane = GROUP * chunk + sub
+            plane = GROUP * chunk + SHIFT + sub
             for r0 in range(0, lines, BLOCK):
                 rows = pl.ds(r0, BLOCK)
                 density, x_mom, y_mom, z_mom, energy = [
@@ -319,22 +355,24 @@
                 columns = pl.ds(pl.multiple_of((2 + seg) * radii, 128), radii)
                 for k in range(FIELDS):
                     high, low = split(radial[k] * scaled_radius)
-                    operand_hi[chunk, k, sub, rows, columns] = high
-                    operand_lo[chunk, k, sub, rows, columns] = low
-                    angular[chunk, seg, k, sub, pl.ds(PAD + r0, BLOCK), :] = around[k]
-                    axial[stage, seg, k, 2 + plane, rows, :] = along[k]
-            slot = stage * chunks + chunk
+                    operand_hi[held, k, sub, rows, columns] = high
+                    operand_lo[held, k, sub, rows, columns] = low
+                    angular[held, seg, k, sub, pl.ds(PAD + r0, BLOCK), :] = around[k]
+                    axial[stage, seg, k, plane, rows, :] = along[k]
             for k in range(FIELDS):
-                edge_out[slot, 0, seg, k, sub] = angular[chunk, seg, k, sub, pl.ds(PAD, 2), :]
+                edge_out[slot, 0, seg, k, sub] = angular[held, seg, k, sub, pl.ds(PAD, 2), :]
                 edge_out[slot, 1, seg, k, sub] = angular[
-                    chunk, seg, k, sub, pl.ds(PAD + lines - 2, 2), :
+                    held, seg, k, sub, pl.ds(PAD + lines - 2, 2), :
                 ]
             return carry
 
         lax.fori_loop(0, 2 * GROUP, one, 0)
-        slot = stage * chunks + chunk
-        edge_copy(0, slot).start()
-        edge_copy(1, slot).start()
+        inside = (chunk >= 0) & (chunk < chunks)
+
+        @pl.when(inside | ((stage == 0) & (chunk == near)))
+        def _():
+            edge_copy(0, slot).start()
+            edge_copy(1, slot).start()
 
         @pl.when((chunk == 0) & has_low)
         def _():
@@ -345,17 +383,18 @@
             axial_copy(1, stage).start()
 
     def advance(stage, chunk):
-        slot = stage * chunks + chunk
+        held = held_at(chunk)
+        slot = slot_of(stage, chunk)
         wait_for(edge_in.at[slot, 0], edge_r.at[slot, 0])
         wait_for(edge_in.at[slot, 1], edge_r.at[slot, 1])
 
         @pl.when((chunk == 0) & has_low)
         def _():
-            wait_for(axial.at[stage, :, :, pl.ds(0, 2)], ax_r.at[stage, 0])
+            wait_for(axial.at[stage, :, :, pl.ds(SHIFT - 2, 2)], ax_r.at[stage, 0])
 
         @pl.when((chunk == chunks - 1) & has_up)
         def _():
-            wait_for(axial.at[stage, :, :, pl.ds(own + 2, 2)], ax_r.at[stage, 1])
+            wait_for(axial.at[stage, :, :, pl.ds(SHIFT + own, 2)], ax_r.at[stage, 1])
 
         factor = (1.0 - 0.5 * stage.astype(jnp.float32)) * COURANT
         turn_near = factor * (twist * 8.0 / 12.0)
@@ -368,21 +407,21 @@
         def one(item, carry):
             seg = lax.div(item, GROUP)
             sub = lax.rem(item, GROUP)
-            plane = GROUP * chunk + sub
+            plane = GROUP * chunk + SHIFT + sub
             seg_low = lax.rem(seg + swap_low, 2)
             seg_up = lax.rem(seg + swap_up, 2)
             for k in range(FIELDS):
-                angular[chunk, seg, k, sub, pl.ds(PAD - 2, 2), :] = edge_in[slot, 0, seg_low, k, sub]
-                angular[chunk, seg, k, sub, pl.ds(PAD + lines, 2), :] = edge_in[slot, 1, seg_up, k, sub]
+                angular[held, seg, k, sub, pl.ds(PAD - 2, 2), :] = edge_in[slot, 0, seg_low, k, sub]
+                angular[held, seg, k, sub, pl.ds(PAD + lines, 2), :] = edge_in[slot, 1, seg_up, k, sub]
             columns = pl.ds(pl.multiple_of(seg * radii, 128), radii)
             for r0 in range(0, lines, BLOCK):
                 rows = pl.ds(r0, BLOCK)
                 for k in range(FIELDS):
                     def beside(offset):
-                        return angular[chunk, seg, k, sub, pl.ds(PAD + r0 + offset, BLOCK), :]
+                        return angular[held, seg, k, sub, pl.ds(PAD + r0 + offset, BLOCK), :]
 
                     def above(offset):
-                        return axial[stage, seg, k, 2 + plane + offset, rows, :]
+                        return axial[stage, seg, k, plane + offset, rows, :]
 
                     base = 0.5 * state[0, seg, k, plane, rows, :] + 0.5 * state[stage, seg, k, plane, rows, :]
                     local = (
@@ -391,37 +430,46 @@
                         - (scaled_near * (above(1) - above(-1)) - scaled_far * (above(2) - above(-2)))
                     )
                     high, low = split(local)
-                    operand_hi[chunk, k, sub, rows, columns] = high
-                    operand_lo[chunk, k, sub, rows, columns] = low
+                    operand_hi[held, k, sub, rows, columns] = high
+                    operand_lo[held, k, sub, rows, columns] = low
             return carry
 
         lax.fori_loop(0, 2 * GROUP, one, 0)
         flat = (FIELDS * GROUP * lines, 4 * radii)
-        high = operand_hi[chunk].reshape(flat)
-        low = operand_lo[chunk].reshape(flat)
+        high = operand_hi[held].reshape(flat)
+        low = operand_lo[held].reshape(flat)
         result = dot(high, gain_hi[...]) + dot(low, gain_hi[...]) + dot(high, gain_lo[...])
         result = result.reshape(FIELDS, GROUP, lines, 2 * radii)
         for seg in range(2):
-            state[stage + 1, seg, :, group(GROUP * chunk)] = result[..., seg * radii : (seg + 1) * radii]
+            state[1 - stage, seg, :, within(chunk)] = result[..., seg * radii : (seg + 1) * radii]
 
     kinds = [kind for kind, _ in steps]
     which = [chunk for _, chunk in steps]
 
     def one_step(step, carry):
         kind = chosen(step, kinds)
-        chunk = chosen(step, which)
-
-        @pl.when(kind == ARRIVE)
-        def _():
-            here = state.at[0, 0, :, group(GROUP * chunk)]
+        label = chosen(step, which)
+        chunk = jnp.where(label == FAR, far, jnp.where(label == NEAR, near, label))
+        usual = label < FAR
+        taken = usual | is_giver
+
+        @pl.when((kind == ARRIVE) & usual)
+        def _():
+            here = state.at[0, 0, :, within(chunk)]
             wait_for(here, in_r.at[0, chunk])
             wait_for(here, in_r.at[1, chunk])
 
-        @pl.when(kind != ARRIVE)
+        @pl.when((label == FAR) & is_giver)
+        def _():
+            here = state.at[0, 0, :, pl.ds(0, more)]
+            wait_for(here, more_r.at[0])
+            wait_for(here, more_r.at[1])
+
+        @pl.when((kind != ARRIVE) & taken)
         def _():
             advance(kind - FIRST, chunk)
 
-        @pl.when(kind != SECOND)
+        @pl.when((kind != SECOND) & taken)
         def _():
             fluxes(kind, chunk)
 
@@ -442,7 +490,7 @@
     lax.fori_loop(0, len(steps), one_step, 0)
 
     def finish(chunk, carry):
-        sample = state.at[0, 0, :, group(GROUP * chunk)]
+        sample = state.at[0, 0, :, within(chunk)]
         wait_for(sample, in_s.at[0, chunk])
         wait_for(sample, out_s.at[0, chunk])
 
@@ -452,7 +500,7 @@
             wait_for(sample, out_s.at[1, chunk])
 
         for stage in range(2):
-            slot = stage * chunks + chunk
+            slot = slot_of(stage, chunk)
             wait_for(edge_out.at[slot, 0], edge_s.at[slot, 0])
             wait_for(edge_out.at[slot, 1], edge_s.at[slot, 1])
         for source in range(2):
@@ -460,14 +508,26 @@
         return carry
 
     lax.fori_loop(0, chunks, finish, 0)
+    sample = state.at[0, 0, :, pl.ds(0, more)]
+
+    @pl.when(is_keeper)
+    def _():
+        wait_for(sample, more_s.at[0])
+
+    @pl.when(is_giver)
+    def _():
+        slot = slot_of(0, near)
+        wait_for(edge_out.at[slot, 0], edge_s.at[slot, 0])
+        wait_for(edge_out.at[slot, 1], edge_s.at[slot, 1])
+
     for stage in range(2):
         @pl.when(has_low)
         def _():
-            wait_for(axial.at[stage, :, :, pl.ds(2, 2)], ax_s.at[stage, 0])
+            wait_for(axial.at[stage, :, :, pl.ds(SHIFT, 2)], ax_s.at[stage, 0])
 
         @pl.when(has_up)
         def _():
-            wait_for(axial.at[stage, :, :, pl.ds(own, 2)], ax_s.at[stage, 1])
+            wait_for(axial.at[stage, :, :, pl.ds(SHIFT + own - 2, 2)], ax_s.at[stage, 1])
 
 
 def per_device(conserved, deriv_matrix, filter_matrix):
@@ -483,27 +543,31 @@
         jet_kernel(n_ang, n_ax, *refs)
 
     dma = pltpu.SemaphoreType.DMA
+    slots = chunks + 2
+    wide = own + 2 * SHIFT
     return pl.pallas_call(
         kernel,
-        out_shape=jax.ShapeDtypeStruct(conserved.shape, f32),
+        out_shape=pltpu.VMEM(conserved.shape, f32),
         in_specs=[anywhere] * 3,
-        out_specs=anywhere,
+        out_specs=pl.BlockSpec(memory_space=pltpu.VMEM),
         scratch_shapes=[
-            pltpu.VMEM((3, 2, FIELDS, own, lines, radii), f32),
-            pltpu.VMEM((chunks, FIELDS, GROUP, lines, 4 * radii), bf16),
-            pltpu.VMEM((chunks, FIELDS, GROUP, lines, 4 * radii), bf16),
-            pltpu.VMEM((chunks, 2, FIELDS, GROUP, lines + 2 * PAD, radii), f32),
-            pltpu.VMEM((2, 2, FIELDS, own + 4, lines, radii), f32),
-            pltpu.VMEM((2 * chunks, 2, 2, FIELDS, GROUP, 2, radii), f32),
-            pltpu.VMEM((2 * chunks, 2, 2, FIELDS, GROUP, 2, radii), f32),
+            pltpu.VMEM((2, 2, FIELDS, wide, lines, radii), f32),
+            pltpu.VMEM((slots, FIELDS, GROUP, lines, 4 * radii), bf16),
+            pltpu.VMEM((slots, FIELDS, GROUP, lines, 4 * radii), bf16),
+            pltpu.VMEM((slots, 2, FIELDS, GROUP, lines + 2 * PAD, radii), f32),
+            pltpu.VMEM((2, 2, FIELDS, wide, lines, radii), f32),
+            pltpu.VMEM((2 * slots, 2, 2, FIELDS, GROUP, 2, radii), f32),
+            pltpu.VMEM((2 * slots, 2, 2, FIELDS, GROUP, 2, radii), f32),
             pltpu.VMEM((2, 2 * radii, 2 * radii), f32),
             pltpu.VMEM((2, 2, lines, 128), f32),
             pltpu.VMEM((4 * radii, 2 * radii), bf16),
             pltpu.VMEM((4 * radii, 2 * radii), bf16),
             dma((2, chunks)),
             dma((2, chunks)),
-            dma((2 * chunks, 2)),
-            dma((2 * chunks, 2)),
+            dma((1,)),
+            dma((2,)),
+            dma((2 * slots, 2)),
+            dma((2 * slots, 2)),
             dma((2, 2)),
             dma((2, 2)),
             dma((2, chunks)),
@@ -511,7 +575,7 @@
             dma((2,)),
         ],
         compiler_params=pltpu.CompilerParams(
-            collective_id=0, has_side_effects=True, vmem_limit_bytes=58 * 1024 * 1024
+            collective_id=0, has_side_effects=True, vmem_limit_bytes=55 * 1024 * 1024
         ),
     )(conserved, deriv_matrix, filter_matrix)
 

time: 129 us -> 115 us (0.89)
  Pallas kernels: 124 us -> 113 us
  local copies, waits for them, and re-layouts: 4.58 us -> 1.93 us
    pallas_call x1, Pallas kernels: 124 us -> 113 us  [per_device(): pl.pallas_call(kernel, out_shape=pltpu.VMEM(conserved.shape, f32), in_spe...]
    unnamed x1, local copies, waits for them, and re-layouts: 4.58 us -> 1.93 us
where the time goes in v1:
time: 115 us
  Pallas kernels  113 us (98%)
  local copies, waits for them, and re-layouts  1.93 us (2%)
    pallas_call x1, Pallas kernels, per_device(): pl.pallas_call(kernel, out_shape=pltpu.VMEM(conserved.shape, f32), in_spe...  113 us

profile of v1, /device:TPU:1, one launch (start us, length us, event | category | flops | bytes accessed | tf_op | source)
XLA Modules:
  0.0 115.1 jit_solution(1520561693521460682)
XLA Ops:
  0.0 113.2 %shard_map.37 = f32[5,24,32,256]{3,2,1,0:T(8,128)S(1)} custom-call(f32[5,24,32,256]{3,2,1,0:T(8,128)} %refs_0_.1, f32[512,512]{1,0:T(8,128)} %refs_1_.1, f32[512,512]{1,0:T(8,128)} %refs_2_.1), custom_call_target="tpu_custom_call" | custom-call | tf_op jit(solution)/shard_map/pallas_call | solution.py:548
  113.2 1.9 %copy.5 = f32[5,24,32,256]{3,2,1,0:T(8,128)} copy(f32[5,24,32,256]{3,2,1,0:T(8,128)S(1)} %shard_map.37) | data formatting | bytes 7864320

commit v2 on v1

--- a/solution.py
+++ b/solution.py
@@ -14,9 +14,10 @@
 BLOCK = 16
 PAD = 8
 SHIFT = 2 * GROUP
+ROW = 8
 
 ARRIVE, FIRST, SECOND = 0, 1, 2
-FAR, NEAR = 100, 101
+FAR, NEAR, BASE = 100, 101, 200
 
 
 def step_list(chunks):
@@ -26,21 +27,44 @@
     def ready(chunk, done):
         return all(n in done for n in (chunk - 1, chunk, chunk + 1) if 0 <= n < chunks)
 
-    for place, chunk in enumerate(order):
+    for turn, chunk in enumerate(order):
         steps.append((ARRIVE, chunk))
         here.add(chunk)
-        if place == 1:
-            steps += [(ARRIVE, FAR), (ARRIVE, NEAR), (FIRST, NEAR)]
-        for c in range(chunks):
+        if turn == 1:
+            steps += [(ARRIVE, FAR), (ARRIVE, NEAR)]
+        for c in sorted(range(chunks), key=lambda c: c == chunk):
             if c not in first and ready(c, here):
                 steps.append((FIRST, c))
                 first.append(c)
-        for c in range(1, chunks - 1):
-            if place < chunks - 1 and c not in second and ready(c, first):
-                steps.append((SECOND, c))
-                second.append(c)
-    late = [c for c in range(1, chunks) if c not in second] + [0]
-    return order, steps + [(SECOND, c) for c in late]
+                if len(first) == 2:
+                    steps.append((FIRST, NEAR))
+                for d in range(1, chunks - 2):
+                    if d not in second and ready(d, first):
+                        steps.append((SECOND, d))
+                        second.append(d)
+    late = list(range(1, chunks - 2)) + [chunks - 1, 0, chunks - 2]
+    return order, steps + [(SECOND, c) for c in late if c not in second]
+
+
+def pass_list(steps):
+    passes = [[], []]
+    for lane in passes:
+        lane += [0] * len(steps)
+    for sent, (kind, label) in enumerate(steps):
+        if kind == SECOND or label == FAR or (kind == FIRST and label == NEAR):
+            continue
+        needed = steps.index((kind + 1, label))
+        middle = sent + 2
+        for lane, at in sorted(
+            ((lane, at) for lane in range(2) for at in range(sent + 1, needed + 1)),
+            key=lambda choice: (choice[0], abs(choice[1] - middle)),
+        ):
+            if not passes[lane][at]:
+                passes[lane][at] = 1 + BASE * kind + label
+                break
+        else:
+            raise ValueError(steps)
+    return passes
 
 
 def chosen(step, values):
@@ -64,8 +88,8 @@
 def jet_kernel(
     n_ang, n_ax, x_ref, deriv_ref, filt_ref, out_ref,
     state, operand_hi, operand_lo, angular, axial, edge_out, edge_in,
-    mats, table, gain_hi, gain_lo,
-    in_s, in_r, more_s, more_r, edge_s, edge_r, ax_s, ax_r, out_s, out_r, mat_s,
+    relayed, mats, table, gain_hi, gain_lo,
+    in_s, in_r, more_s, more_r, edge_s, edge_r, relay_s, relay_r, ax_s, ax_r, out_s, out_r, mat_s,
 ):
     planes, lines, radii = x_ref.shape[1:]
     own = planes // 2
@@ -73,6 +97,7 @@
     half = n_ang // 2
     n_hi = n_ax // 2
     order, steps = step_list(chunks)
+    passes = pass_list(steps)
 
     ang = lax.axis_index("ang")
     ax = lax.axis_index("ax")
@@ -88,6 +113,20 @@
     left = (side * half + lax.rem(place + half - 1, half), ax)
     right = (side * half + lax.rem(place + 1, half), ax)
 
+    n_rows = half // ROW
+    relays = n_rows > 1
+    row = lax.div(place, ROW)
+    column = lax.rem(place, ROW)
+    ends_row = (column == 0, column == ROW - 1)
+    beside_end = (column == 1, column == ROW - 2)
+    is_relay = beside_end[0] | beside_end[1]
+    to_right = jnp.where(beside_end[1], jnp.int32(1), jnp.int32(0))
+
+    def at_place(row_number, column_number):
+        return (side * half + lax.rem(row_number + n_rows, n_rows) * ROW + column_number, ax)
+
+    relay_target = at_place(row + 2 * to_right - 1, jnp.where(beside_end[1], 0, ROW - 1))
+
     low_sib = core == 1
     low_far = (core == 0) & (keep == 1)
     low_z = (core == 0) & (keep == 0) & (z_hi > 0)
@@ -174,6 +213,51 @@
             device_id_type=MESH,
         )
 
+    def edge_half(which, slot, seg):
+        return pltpu.make_async_remote_copy(
+            src_ref=edge_out.at[slot, which, seg],
+            dst_ref=edge_in.at[slot, 1 - which, seg],
+            send_sem=edge_s.at[slot, which],
+            recv_sem=edge_r.at[slot, 1 - which],
+            device_id=left if which == 0 else right,
+            device_id_type=MESH,
+        )
+
+    def edge_to_relay(which, slot, seg):
+        return pltpu.make_async_remote_copy(
+            src_ref=edge_out.at[slot, which, seg],
+            dst_ref=relayed.at[slot],
+            send_sem=edge_s.at[slot, which],
+            recv_sem=relay_r.at[slot],
+            device_id=right if which == 0 else left,
+            device_id_type=MESH,
+        )
+
+    def edge_from_relay(slot, seg):
+        return pltpu.make_async_remote_copy(
+            src_ref=relayed.at[slot],
+            dst_ref=edge_in.at[slot, 1 - to_right, seg],
+            send_sem=relay_s.at[slot],
+            recv_sem=edge_r.at[slot, 1 - to_right],
+            device_id=relay_target,
+            device_id_type=MESH,
+        )
+
+    def send_edges(slot):
+        for direction in range(2):
+            if not relays:
+                edge_copy(direction, slot).start()
+                continue
+
+            @pl.when(jnp.logical_not(ends_row[direction]))
+            def _():
+                edge_copy(direction, slot).start()
+
+            @pl.when(ends_row[direction])
+            def _():
+                edge_to_relay(direction, slot, 1).start()
+                edge_half(direction, slot, 0).start()
+
     def axial_copy(which, stage):
         if which == 0:
             source, target, device = SHIFT, SHIFT + own, low_dev
@@ -228,7 +312,16 @@
     def _():
         pl.semaphore_signal(barrier, inc=1, device_id=up_dev, device_id_type=MESH)
 
-    pl.semaphore_wait(barrier, jnp.where(low_z | up_z, jnp.int32(6), jnp.int32(5)))
+    arrivals = jnp.where(low_z | up_z, jnp.int32(6), jnp.int32(5))
+    if relays:
+        for direction in range(2):
+            @pl.when(ends_row[1 - direction])
+            def _():
+                device = at_place(row + 1 - 2 * direction, ROW - 2 if direction else 1)
+                pl.semaphore_signal(barrier, inc=1, device_id=device, device_id_type=MESH)
+
+        arrivals = arrivals + jnp.where(is_relay, jnp.int32(1), jnp.int32(0))
+    pl.semaphore_wait(barrier, arrivals)
 
     @pl.when(is_giver)
     def _():
@@ -266,9 +359,9 @@
         table[seg, 0] = jnp.cos(angle)
         table[seg, 1] = jnp.sin(angle)
 
-    row = lax.broadcasted_iota(jnp.int32, (radii, radii), 0)
-    column = lax.broadcasted_iota(jnp.int32, (radii, radii), 1)
-    flip = jnp.where(row + column == radii - 1, 1.0, 0.0).astype(jnp.bfloat16)
+    down = lax.broadcasted_iota(jnp.int32, (radii, radii), 0)
+    over = lax.broadcasted_iota(jnp.int32, (radii, radii), 1)
+    flip = jnp.where(down + over == radii - 1, 1.0, 0.0).astype(jnp.bfloat16)
 
     def arranged(part):
         low_rows = dot(flip, part[:radii]).astype(jnp.bfloat16)
@@ -371,8 +464,7 @@
 
         @pl.when(inside | ((stage == 0) & (chunk == near)))
         def _():
-            edge_copy(0, slot).start()
-            edge_copy(1, slot).start()
+            send_edges(slot)
 
         @pl.when((chunk == 0) & has_low)
         def _():
@@ -446,7 +538,24 @@
     kinds = [kind for kind, _ in steps]
     which = [chunk for _, chunk in steps]
 
+    def pass_on(code):
+        stage = lax.div(code - 1, BASE)
+        label = lax.rem(code - 1, BASE)
+        held = held_at(jnp.where(label == NEAR, near, label))
+        slot = stage * (chunks + 2) + held
+        sent = (code > 0) & ((label != NEAR) | is_giver)
+
+        @pl.when(sent & is_relay)
+        def _():
+            wait_for(relayed.at[slot], relay_r.at[slot])
+            edge_from_relay(slot, 1).start()
+
     def one_step(step, carry):
+        if relays:
+            for lane in passes:
+                if any(lane):
+                    pass_on(chosen(step, lane))
+
         kind = chosen(step, kinds)
         label = chosen(step, which)
         chunk = jnp.where(label == FAR, far, jnp.where(label == NEAR, near, label))
@@ -503,6 +612,11 @@
             slot = slot_of(stage, chunk)
             wait_for(edge_out.at[slot, 0], edge_s.at[slot, 0])
             wait_for(edge_out.at[slot, 1], edge_s.at[slot, 1])
+            if relays:
+                @pl.when(is_relay)
+                def _():
+                    wait_for(relayed.at[slot], relay_s.at[slot])
+
         for source in range(2):
             wait_for(sample, out_r.at[source, chunk])
         return carry
@@ -519,6 +633,10 @@
         slot = slot_of(0, near)
         wait_for(edge_out.at[slot, 0], edge_s.at[slot, 0])
         wait_for(edge_out.at[slot, 1], edge_s.at[slot, 1])
+        if relays:
+            @pl.when(is_relay)
+            def _():
+                wait_for(relayed.at[slot], relay_s.at[slot])
 
     for stage in range(2):
         @pl.when(has_low)
@@ -558,6 +676,7 @@
             pltpu.VMEM((2, 2, FIELDS, wide, lines, radii), f32),
             pltpu.VMEM((2 * slots, 2, 2, FIELDS, GROUP, 2, radii), f32),
             pltpu.VMEM((2 * slots, 2, 2, FIELDS, GROUP, 2, radii), f32),
+            pltpu.VMEM((2 * slots, FIELDS, GROUP, 2, radii), f32),
             pltpu.VMEM((2, 2 * radii, 2 * radii), f32),
             pltpu.VMEM((2, 2, lines, 128), f32),
             pltpu.VMEM((4 * radii, 2 * radii), bf16),
@@ -568,6 +687,8 @@
             dma((2,)),
             dma((2 * slots, 2)),
             dma((2 * slots, 2)),
+            dma((2 * slots,)),
+            dma((2 * slots,)),
             dma((2, 2)),
             dma((2, 2)),
             dma((2, chunks)),

time: 115 us -> 111 us (0.965); the launches traced: 115 us -> 110 us
  Pallas kernels: 113 us -> 108 us
    pallas_call x1, Pallas kernels: 113 us -> 108 us  [per_device(): pl.pallas_call(kernel, out_shape=pltpu.VMEM(conserved.shape, f32), in_spe...]
where the time goes in v2:
time: 111 us; the launch traced here: 110 us
  Pallas kernels  108 us (97%)
  local copies, waits for them, and re-layouts  1.93 us (2%)
    pallas_call x1, Pallas kernels, per_device(): pl.pallas_call(kernel, out_shape=pltpu.VMEM(conserved.shape, f32), in_spe...  108 us

profile of v2, /device:TPU:1, one launch (start us, length us, event | category | flops | bytes accessed | tf_op | source)
XLA Modules:
  0.0 109.6 jit_solution(15871452298089464127)
XLA Ops:
  0.0 107.7 %shard_map.37 = f32[5,24,32,256]{3,2,1,0:T(8,128)S(1)} custom-call(f32[5,24,32,256]{3,2,1,0:T(8,128)} %refs_0_.1, f32[512,512]{1,0:T(8,128)} %refs_1_.1, f32[512,512]{1,0:T(8,128)} %refs_2_.1), custom_call_target="tpu_custom_call" | custom-call | tf_op jit(solution)/shard_map/pallas_call | solution.py:666
  107.7 1.9 %copy.5 = f32[5,24,32,256]{3,2,1,0:T(8,128)} copy(f32[5,24,32,256]{3,2,1,0:T(8,128)S(1)} %shard_map.37) | data formatting | bytes 7864320

commit v3 on v2

--- a/solution.py
+++ b/solution.py
@@ -15,6 +15,7 @@
 PAD = 8
 SHIFT = 2 * GROUP
 ROW = 8
+DETOUR = 2
 
 ARRIVE, FIRST, SECOND = 0, 1, 2
 FAR, NEAR, BASE = 100, 101, 200
@@ -30,7 +31,7 @@
     for turn, chunk in enumerate(order):
         steps.append((ARRIVE, chunk))
         here.add(chunk)
-        if turn == 1:
+        if turn == 2:
             steps += [(ARRIVE, FAR), (ARRIVE, NEAR)]
         for c in sorted(range(chunks), key=lambda c: c == chunk):
             if c not in first and ready(c, here):
@@ -88,8 +89,8 @@
 def jet_kernel(
     n_ang, n_ax, x_ref, deriv_ref, filt_ref, out_ref,
     state, operand_hi, operand_lo, angular, axial, edge_out, edge_in,
-    relayed, mats, table, gain_hi, gain_lo,
-    in_s, in_r, more_s, more_r, edge_s, edge_r, relay_s, relay_r, ax_s, ax_r, out_s, out_r, mat_s,
+    relayed, detoured, mats, table, gain_hi, gain_lo,
+    in_s, in_r, more_s, more_r, detour_s, detour_r, edge_s, edge_r, relay_s, relay_r, ax_s, ax_r, out_s, out_r, mat_s,
 ):
     planes, lines, radii = x_ref.shape[1:]
     own = planes // 2
@@ -109,6 +110,9 @@
     is_keeper = core == keep
     is_giver = core != keep
     across = lax.rem(ang + half, n_ang)
+    def across_of_side(position):
+        return (1 - side) * half + position
+
     sibling = (ang, 2 * z_hi + 1 - core)
     left = (side * half + lax.rem(place + half - 1, half), ax)
     right = (side * half + lax.rem(place + 1, half), ax)
@@ -124,6 +128,18 @@
 
     def at_place(row_number, column_number):
         return (side * half + lax.rem(row_number + n_rows, n_rows) * ROW + column_number, ax)
+
+    detours = relays and ROW >= 8
+    low_end, high_end = column < 2, column >= ROW - 2
+    low_beside = (column == 2) | (column == 3)
+    high_beside = (column == ROW - 4) | (column == ROW - 3)
+    is_detoured = low_end | high_end
+    is_detour = low_beside | high_beside
+    outward = jnp.where(low_end | low_beside, jnp.int32(-2), jnp.int32(2))
+    inward_across = across_of_side(place - outward)
+    outward_across = across_of_side(place + outward)
+    inward_here = side * half + place - outward
+    outward_here = side * half + place + outward
 
     relay_target = at_place(row + 2 * to_right - 1, jnp.where(beside_end[1], 0, ROW - 1))
 
@@ -190,15 +206,49 @@
             more_r.at[0],
         )
 
-    def more_across():
-        return pltpu.make_async_remote_copy(
-            src_ref=x_ref.at[:, pl.ds(first_more, more)],
-            dst_ref=state.at[0, side, :, pl.ds(place_more, more)],
+    def more_fields(first, count, device):
+        return pltpu.make_async_remote_copy(
+            src_ref=x_ref.at[pl.ds(first, count), pl.ds(first_more, more)],
+            dst_ref=state.at[0, side, pl.ds(first, count), pl.ds(place_more, more)],
+            send_sem=more_s.at[1 if first else 0],
+            recv_sem=more_r.at[2 if first else 1],
+            device_id=(device, ax),
+            device_id_type=MESH,
+        )
+
+    def more_to_detour():
+        return pltpu.make_async_remote_copy(
+            src_ref=x_ref.at[pl.ds(0, DETOUR), pl.ds(first_more, more)],
+            dst_ref=detoured,
             send_sem=more_s.at[0],
+            recv_sem=detour_r.at[0],
+            device_id=(inward_across, ax),
+            device_id_type=MESH,
+        )
+
+    def more_from_detour():
+        return pltpu.make_async_remote_copy(
+            src_ref=detoured,
+            dst_ref=state.at[0, 1 - side, pl.ds(0, DETOUR), pl.ds(place_more, more)],
+            send_sem=detour_s.at[0],
             recv_sem=more_r.at[1],
-            device_id=(across, ax),
-            device_id_type=MESH,
-        )
+            device_id=(outward_here, ax),
+            device_id_type=MESH,
+        )
+
+    def send_more():
+        more_fields(DETOUR, FIELDS - DETOUR, across).start()
+        if not detours:
+            more_fields(0, DETOUR, across).start()
+            return
+
+        @pl.when(is_detoured)
+        def _():
+            more_to_detour().start()
+
+        @pl.when(jnp.logical_not(is_detoured))
+        def _():
+            more_fields(0, DETOUR, across).start()
 
     def wait_for(ref, sem):
         pltpu.make_async_copy(ref, ref, sem).wait()
@@ -321,6 +371,19 @@
                 pl.semaphore_signal(barrier, inc=1, device_id=device, device_id_type=MESH)
 
         arrivals = arrivals + jnp.where(is_relay, jnp.int32(1), jnp.int32(0))
+    if detours:
+        @pl.when(is_giver & is_detoured)
+        def _():
+            device = (inward_here, ax)
+            pl.semaphore_signal(barrier, inc=1, device_id=device, device_id_type=MESH)
+
+        @pl.when(is_giver & is_detour)
+        def _():
+            device = (outward_across, ax)
+            pl.semaphore_signal(barrier, inc=1, device_id=device, device_id_type=MESH)
+
+        more_peers = (is_keeper & is_detoured) | (is_giver & is_detour)
+        arrivals = arrivals + jnp.where(more_peers, jnp.int32(1), jnp.int32(0))
     pl.semaphore_wait(barrier, arrivals)
 
     @pl.when(is_giver)
@@ -328,16 +391,15 @@
         for turn, chunk in enumerate(order):
             for target in range(2):
                 give(target, chunk).start()
-            if turn == 1:
+            if turn == 0:
                 more_here().start()
 
     @pl.when(is_keeper)
     def _():
-        for turn, chunk in enumerate(order):
+        send_more()
+        for chunk in order:
             hold(chunk).start()
             share(chunk).start()
-            if turn == 1:
-                more_across().start()
 
     for copy in load_mats():
         copy.start()
@@ -555,6 +617,11 @@
             for lane in passes:
                 if any(lane):
                     pass_on(chosen(step, lane))
+        if detours:
+            @pl.when((step == steps.index((ARRIVE, order[2]))) & is_giver & is_detour)
+            def _():
+                wait_for(detoured, detour_r.at[0])
+                more_from_detour().start()
 
         kind = chosen(step, kinds)
         label = chosen(step, which)
@@ -570,9 +637,9 @@
 
         @pl.when((label == FAR) & is_giver)
         def _():
-            here = state.at[0, 0, :, pl.ds(0, more)]
-            wait_for(here, more_r.at[0])
-            wait_for(here, more_r.at[1])
+            wait_for(state.at[0, 0, :, pl.ds(0, more)], more_r.at[0])
+            wait_for(state.at[0, 0, pl.ds(0, DETOUR), pl.ds(0, more)], more_r.at[1])
+            wait_for(state.at[0, 0, pl.ds(DETOUR, FIELDS - DETOUR), pl.ds(0, more)], more_r.at[2])
 
         @pl.when((kind != ARRIVE) & taken)
         def _():
@@ -622,11 +689,15 @@
         return carry
 
     lax.fori_loop(0, chunks, finish, 0)
-    sample = state.at[0, 0, :, pl.ds(0, more)]
-
     @pl.when(is_keeper)
     def _():
-        wait_for(sample, more_s.at[0])
+        wait_for(state.at[0, 0, pl.ds(0, DETOUR), pl.ds(0, more)], more_s.at[0])
+        wait_for(state.at[0, 0, pl.ds(DETOUR, FIELDS - DETOUR), pl.ds(0, more)], more_s.at[1])
+
+    if detours:
+        @pl.when(is_giver & is_detour)
+        def _():
+            wait_for(detoured, detour_s.at[0])
 
     @pl.when(is_giver)
     def _():
@@ -677,14 +748,17 @@
             pltpu.VMEM((2 * slots, 2, 2, FIELDS, GROUP, 2, radii), f32),
             pltpu.VMEM((2 * slots, 2, 2, FIELDS, GROUP, 2, radii), f32),
             pltpu.VMEM((2 * slots, FIELDS, GROUP, 2, radii), f32),
+            pltpu.VMEM((DETOUR, 2 * GROUP, lines, radii), f32),
             pltpu.VMEM((2, 2 * radii, 2 * radii), f32),
             pltpu.VMEM((2, 2, lines, 128), f32),
             pltpu.VMEM((4 * radii, 2 * radii), bf16),
             pltpu.VMEM((4 * radii, 2 * radii), bf16),
             dma((2, chunks)),
             dma((2, chunks)),
+            dma((2,)),
+            dma((3,)),
             dma((1,)),
-            dma((2,)),
+            dma((1,)),
             dma((2 * slots, 2)),
             dma((2 * slots, 2)),
             dma((2 * slots,)),

time: 111 us -> 109 us (0.982)
  Pallas kernels: 108 us -> 105 us
    pallas_call x1, Pallas kernels: 108 us -> 105 us  [per_device(): pl.pallas_call(kernel, out_shape=pltpu.VMEM(conserved.shape, f32), in_spe...]
where the time goes in v3:
time: 109 us; the launch traced here: 107 us
  Pallas kernels  105 us (96%)
  local copies, waits for them, and re-layouts  1.93 us (2%)
    pallas_call x1, Pallas kernels, per_device(): pl.pallas_call(kernel, out_shape=pltpu.VMEM(conserved.shape, f32), in_spe...  105 us

profile of v3, /device:TPU:1, one launch (start us, length us, event | category | flops | bytes accessed | tf_op | source)
XLA Modules:
  0.0 106.8 jit_solution(9438680959083045123)
XLA Ops:
  0.0 104.9 %shard_map.37 = f32[5,24,32,256]{3,2,1,0:T(8,128)S(1)} custom-call(f32[5,24,32,256]{3,2,1,0:T(8,128)} %refs_0_.1, f32[512,512]{1,0:T(8,128)} %refs_1_.1, f32[512,512]{1,0:T(8,128)} %refs_2_.1), custom_call_target="tpu_custom_call" | custom-call | tf_op jit(solution)/shard_map/pallas_call | solution.py:737
  104.9 1.9 %copy.5 = f32[5,24,32,256]{3,2,1,0:T(8,128)} copy(f32[5,24,32,256]{3,2,1,0:T(8,128)S(1)} %shard_map.37) | data formatting | bytes 7864320

commit v4 on v3

--- a/solution.py
+++ b/solution.py
@@ -22,29 +22,17 @@
 
 
 def step_list(chunks):
-    order = [chunks - 1] + list(range(chunks - 1))
-    steps, here, first, second = [], set(), [], []
-
-    def ready(chunk, done):
-        return all(n in done for n in (chunk - 1, chunk, chunk + 1) if 0 <= n < chunks)
-
-    for turn, chunk in enumerate(order):
+    steps = []
+    for chunk in range(chunks):
         steps.append((ARRIVE, chunk))
-        here.add(chunk)
-        if turn == 2:
+        if chunk == chunks // 2:
             steps += [(ARRIVE, FAR), (ARRIVE, NEAR)]
-        for c in sorted(range(chunks), key=lambda c: c == chunk):
-            if c not in first and ready(c, here):
-                steps.append((FIRST, c))
-                first.append(c)
-                if len(first) == 2:
-                    steps.append((FIRST, NEAR))
-                for d in range(1, chunks - 2):
-                    if d not in second and ready(d, first):
-                        steps.append((SECOND, d))
-                        second.append(d)
-    late = list(range(1, chunks - 2)) + [chunks - 1, 0, chunks - 2]
-    return order, steps + [(SECOND, c) for c in late if c not in second]
+        if chunk >= 1:
+            steps.append((FIRST, chunk - 1))
+        if chunk >= 2:
+            steps.append((SECOND, chunk - 2))
+    last = chunks - 1
+    return steps + [(FIRST, last), (FIRST, NEAR), (SECOND, last - 1), (SECOND, last)]
 
 
 def pass_list(steps):
@@ -97,7 +85,7 @@
     chunks = own // GROUP
     half = n_ang // 2
     n_hi = n_ax // 2
-    order, steps = step_list(chunks)
+    steps = step_list(chunks)
     passes = pass_list(steps)
 
     ang = lax.axis_index("ang")
@@ -157,6 +145,10 @@
     far = jnp.where(core == 0, jnp.int32(-2), jnp.int32(chunks + 1))
     more = 2 * GROUP
 
+    def outward_chunk(for_core, turn):
+        return jnp.where(for_core == 1, turn, chunks - 1 - turn)
+
+
     def load_mats():
         return [
             pltpu.make_async_copy(filt_ref, mats.at[0], mat_s.at[0]),
@@ -388,18 +380,17 @@
 
     @pl.when(is_giver)
     def _():
-        for turn, chunk in enumerate(order):
-            for target in range(2):
-                give(target, chunk).start()
-            if turn == 0:
-                more_here().start()
+        more_here().start()
+        for turn in range(chunks):
+            give(0, chunks - 1 - turn).start()
+            give(1, turn).start()
 
     @pl.when(is_keeper)
     def _():
         send_more()
-        for chunk in order:
-            hold(chunk).start()
-            share(chunk).start()
+        for turn in range(chunks):
+            hold(outward_chunk(core, turn)).start()
+            share(outward_chunk(1 - core, turn)).start()
 
     for copy in load_mats():
         copy.start()
@@ -603,8 +594,7 @@
     def pass_on(code):
         stage = lax.div(code - 1, BASE)
         label = lax.rem(code - 1, BASE)
-        held = held_at(jnp.where(label == NEAR, near, label))
-        slot = stage * (chunks + 2) + held
+        slot = slot_of(stage, jnp.where(label == NEAR, near, outward_chunk(core, label)))
         sent = (code > 0) & ((label != NEAR) | is_giver)
 
         @pl.when(sent & is_relay)
@@ -618,14 +608,14 @@
                 if any(lane):
                     pass_on(chosen(step, lane))
         if detours:
-            @pl.when((step == steps.index((ARRIVE, order[2]))) & is_giver & is_detour)
+            @pl.when((step == steps.index((ARRIVE, 2))) & is_giver & is_detour)
             def _():
                 wait_for(detoured, detour_r.at[0])
                 more_from_detour().start()
 
         kind = chosen(step, kinds)
         label = chosen(step, which)
-        chunk = jnp.where(label == FAR, far, jnp.where(label == NEAR, near, label))
+        chunk = jnp.where(label == FAR, far, jnp.where(label == NEAR, near, outward_chunk(core, label)))
         usual = label < FAR
         taken = usual | is_giver
 

time: 109 us -> 107 us (0.982); the launches traced: 107 us -> 107 us
  no operation moved by 1% of the time
where the time goes in v4:
time: 107 us
  Pallas kernels  105 us (98%)
  local copies, waits for them, and re-layouts  1.93 us (2%)
    pallas_call x1, Pallas kernels, per_device(): pl.pallas_call(kernel, out_shape=pltpu.VMEM(conserved.shape, f32), in_spe...  105 us

profile of v4, /device:TPU:1, one launch (start us, length us, event | category | flops | bytes accessed | tf_op | source)
XLA Modules:
  0.0 107.1 jit_solution(4724482959131297281)
XLA Ops:
  0.0 105.2 %shard_map.37 = f32[5,24,32,256]{3,2,1,0:T(8,128)S(1)} custom-call(f32[5,24,32,256]{3,2,1,0:T(8,128)} %refs_0_.1, f32[512,512]{1,0:T(8,128)} %refs_1_.1, f32[512,512]{1,0:T(8,128)} %refs_2_.1), custom_call_target="tpu_custom_call" | custom-call | tf_op jit(solution)/shard_map/pallas_call | solution.py:727
  105.2 1.9 %copy.5 = f32[5,24,32,256]{3,2,1,0:T(8,128)} copy(f32[5,24,32,256]{3,2,1,0:T(8,128)S(1)} %shard_map.37) | data formatting | bytes 7864320

commit v5 on v4

--- a/solution.py
+++ b/solution.py
@@ -15,7 +15,7 @@
 PAD = 8
 SHIFT = 2 * GROUP
 ROW = 8
-DETOUR = 2
+DETOUR = 3
 
 ARRIVE, FIRST, SECOND = 0, 1, 2
 FAR, NEAR, BASE = 100, 101, 200

time: 107 us -> 107 us (level)
  no operation moved by 1% of the time
where the time goes in v5:
time: 107 us; the launch traced here: 106 us
  Pallas kernels  104 us (97%)
  local copies, waits for them, and re-layouts  1.93 us (2%)
    pallas_call x1, Pallas kernels, per_device(): pl.pallas_call(kernel, out_shape=pltpu.VMEM(conserved.shape, f32), in_spe...  104 us

profile of v5, /device:TPU:1, one launch (start us, length us, event | category | flops | bytes accessed | tf_op | source)
XLA Modules:
  0.0 106.1 jit_solution(991325115155164965)
XLA Ops:
  0.0 104.2 %shard_map.37 = f32[5,24,32,256]{3,2,1,0:T(8,128)S(1)} custom-call(f32[5,24,32,256]{3,2,1,0:T(8,128)} %refs_0_.1, f32[512,512]{1,0:T(8,128)} %refs_1_.1, f32[512,512]{1,0:T(8,128)} %refs_2_.1), custom_call_target="tpu_custom_call" | custom-call | tf_op jit(solution)/shard_map/pallas_call | solution.py:727
  104.2 1.9 %copy.5 = f32[5,24,32,256]{3,2,1,0:T(8,128)} copy(f32[5,24,32,256]{3,2,1,0:T(8,128)S(1)} %shard_map.37) | data formatting | bytes 7864320

commit v6 on v4

--- a/solution.py
+++ b/solution.py
@@ -43,7 +43,7 @@
         if kind == SECOND or label == FAR or (kind == FIRST and label == NEAR):
             continue
         needed = steps.index((kind + 1, label))
-        middle = sent + 2
+        middle = sent + 3
         for lane, at in sorted(
             ((lane, at) for lane in range(2) for at in range(sent + 1, needed + 1)),
             key=lambda choice: (choice[0], abs(choice[1] - middle)),

time: 107 us -> 107 us (level)
  no operation moved by 1% of the time
where the time goes in v6:
time: 107 us
  Pallas kernels  105 us (98%)
  local copies, waits for them, and re-layouts  1.93 us (2%)
    pallas_call x1, Pallas kernels, per_device(): pl.pallas_call(kernel, out_shape=pltpu.VMEM(conserved.shape, f32), in_spe...  105 us

profile of v6, /device:TPU:1, one launch (start us, length us, event | category | flops | bytes accessed | tf_op | source)
XLA Modules:
  0.0 106.8 jit_solution(4187730006621458105)
XLA Ops:
  0.0 104.9 %shard_map.37 = f32[5,24,32,256]{3,2,1,0:T(8,128)S(1)} custom-call(f32[5,24,32,256]{3,2,1,0:T(8,128)} %refs_0_.1, f32[512,512]{1,0:T(8,128)} %refs_1_.1, f32[512,512]{1,0:T(8,128)} %refs_2_.1), custom_call_target="tpu_custom_call" | custom-call | tf_op jit(solution)/shard_map/pallas_call | solution.py:727
  104.9 1.9 %copy.5 = f32[5,24,32,256]{3,2,1,0:T(8,128)} copy(f32[5,24,32,256]{3,2,1,0:T(8,128)S(1)} %shard_map.37) | data formatting | bytes 7864320
